TPU v7x, 32 devices: a whole 2x2x4 slice. The times are simulated.
32 devices in a mesh: chan: 4 (over x, core), az: 2 (over y), rng: 4 (over z).
Axes of the slice: x: 2, y: 2, z: 4, core: 2. Of those that a mesh axis runs over, the one named last changes fastest.
Arguments:
- raw: float32 [2, 16, 64, 16384], P(None, 'chan', 'rng', 'az'), may hold values from -6 to 6
- taps: float32 [2, 17, 64], P(None, None, 'rng'), may hold values from -1.5 to 1.5
- recon: float32 [2, 16, 16, 16384], P(None, 'az', None, ('chan', 'rng')), may hold values from -1 to 1
- channel_slot: int32 [16], replicated, may hold values from 0 to 15, each once
Outputs:
- reconstructed: float32 [2, 16, 4, 16, 16384], P(None, None, None, 'az', ('chan', 'rng'))
Inputs may be any that keep to these rules, and one draw needn't show every extreme that they name: `channel_slot`: a permutation of the channels.
All inputs are finite; a program needn't handle non-finite values.
Results may differ from a plain program's by a relative error of at most 0.0003.
Values sent between devices are 32-bit elements; how exact they have to be, the bound alone decides.
No kernel may reach another device: no remote copies, remote signals or barrier semaphores. Data moves between devices by JAX's collectives and lax.ppermute only.
A program may use at most 192 MiB of HBM per device.

v0:
```python
import math
import jax
import jax.numpy as jnp
from jax import lax
from jax.sharding import PartitionSpec as P


def with_halo(shard, sides, width):
    for axis, dim in sides:
        size, length = (lax.axis_size(axis), shard.shape[dim])
        up = [(i, (i + 1) % size) for i in range(size - 1)]
        down = [(j, i) for i, j in up]
        last = lax.slice_in_dim(shard, length - width, length, axis=dim)
        leading = lax.slice_in_dim(shard, 0, width, axis=dim)
        before = lax.ppermute(last, axis, up)
        after = lax.ppermute(leading, axis, down)
        shard = jnp.concatenate([before, shard, after], axis=dim)
    return shard


def phases(first, second, length):
    left = jnp.arange(first, dtype=jnp.int32)
    right = jnp.arange(second, dtype=jnp.int32)
    product = left[:, None] * right[None, :] % length
    angle = product.astype(jnp.float32) * (2.0 * math.pi / length)
    return (jnp.cos(angle), jnp.sin(angle))


def azimuth_fft(block):
    count = block.shape[-1]
    rows = math.isqrt(count)
    while count % rows:
        rows = rows - 1
    cols = count // rows
    lead = block.shape[1:-1]
    high = lax.Precision.HIGHEST
    real_in = block[0].reshape(lead + (rows, cols))
    imag_in = block[1].reshape(lead + (rows, cols))
    cosine_first, sine_first = phases(rows, rows, rows)
    first_real = jnp.einsum("...ab,af->...bf", real_in, cosine_first, precision=high) + jnp.einsum(
        "...ab,af->...bf", imag_in, sine_first, precision=high
    )
    first_imag = jnp.einsum("...ab,af->...bf", imag_in, cosine_first, precision=high) - jnp.einsum(
        "...ab,af->...bf", real_in, sine_first, precision=high
    )
    twist_cos, twist_sin = phases(cols, rows, count)
    turned_real = first_real * twist_cos + first_imag * twist_sin
    turned_imag = first_imag * twist_cos - first_real * twist_sin
    cosine_second, sine_second = phases(cols, cols, cols)
    out_real = jnp.einsum(
        "...bf,bg->...gf", turned_real, cosine_second, precision=high
    ) + jnp.einsum("...bf,bg->...gf", turned_imag, sine_second, precision=high)
    out_imag = jnp.einsum(
        "...bf,bg->...gf", turned_imag, cosine_second, precision=high
    ) - jnp.einsum("...bf,bg->...gf", turned_real, sine_second, precision=high)
    scale = 1.0 / math.sqrt(count)
    return jnp.stack([out_real.reshape(lead + (count,)), out_imag.reshape(lead + (count,))]) * scale


def shards(raw, taps, recon, channel_slot):
    width = taps.shape[1]
    half = (width - 1) // 2
    strip_rows = raw.shape[2]
    padded = with_halo(raw, (("rng", 2),), half)
    real_part = jnp.zeros(raw.shape[1:], jnp.float32)
    imag_part = jnp.zeros(raw.shape[1:], jnp.float32)
    for offset in range(width):
        seg_real = padded[0, :, offset : offset + strip_rows, :]
        seg_imag = padded[1, :, offset : offset + strip_rows, :]
        tap_real = taps[0, offset][None, :, None]
        tap_imag = taps[1, offset][None, :, None]
        real_part = real_part + tap_real * seg_real - tap_imag * seg_imag
        imag_part = imag_part + tap_real * seg_imag + tap_imag * seg_real
    filtered = jnp.stack([real_part, imag_part])
    spectrum = azimuth_fft(lax.all_to_all(filtered, "az", split_axis=2, concat_axis=3, tiled=True))
    strips = lax.axis_size("rng")
    groups = lax.axis_size("chan")
    local_channels = spectrum.shape[1]
    local_range = spectrum.shape[2]
    moved = lax.all_to_all(
        spectrum[:, None], ("chan", "rng"), split_axis=4, concat_axis=1, tiled=True
    )
    bins = moved.shape[-1]
    moved = moved.reshape((2, groups, strips, local_channels, local_range, bins))
    doppler = jnp.transpose(moved, (0, 1, 3, 2, 4, 5)).reshape(
        (2, groups * local_channels, strips * local_range, bins)
    )
    channels = doppler.shape[1]
    selector = (channel_slot[:, None] == jnp.arange(channels, dtype=jnp.int32)[None, :]).astype(
        jnp.float32
    )
    piece = lax.all_gather(recon, "az", axis=1, tiled=True)
    arranged = jnp.einsum("pkjf,cj->pkcf", piece, selector, precision=lax.Precision.HIGHEST)
    shape = (piece.shape[1], doppler.shape[2], doppler.shape[3])
    out_real = jnp.zeros(shape, jnp.float32)
    out_imag = jnp.zeros(shape, jnp.float32)
    for channel in range(channels):
        mat_real = arranged[0, :, channel, None, :]
        mat_imag = arranged[1, :, channel, None, :]
        data_real = doppler[0, channel][None]
        data_imag = doppler[1, channel][None]
        out_real = out_real + mat_real * data_real - mat_imag * data_imag
        out_imag = out_imag + mat_real * data_imag + mat_imag * data_real
    result = jnp.stack([out_real, out_imag])
    total_range = result.shape[2]
    return result.reshape((2, result.shape[1], strips, total_range // strips, result.shape[3]))


def solution(mesh):
    return jax.shard_map(
        shards,
        mesh=mesh,
        in_specs=(
            P(None, "chan", "rng", "az"),
            P(None, None, "rng"),
            P(None, "az", None, ("chan", "rng")),
            P(),
        ),
        out_specs=P(None, None, None, "az", ("chan", "rng")),
        check_vma=False,
    )
```

profile of v0, /device:TPU:0, one launch (start us, length us, event | category | flops | bytes accessed | tf_op | source)
XLA Modules:
  0.0 701.0 jit_solution(1237962557530691339)
XLA Ops:
  9.0 5.1 collective-permute-start
  16.4 42.5 %collective-permute-done = f32[2,4,8,8192]{3,2,1,0:T(8,128)S(1)} collective-permute-done((f32[2,4,8,8192]{3,2,1,0:T(8,128)S(1)}, f32[2,4,8,8192]{3,2,1,0:T(8,128)S(1)}, u32[]{:S(2)}, u32[]{:S(2)}) %collective-permute-start) | collective-permute-done | bytes 2097184 | tf_op jit(solution)/shard_map/ppermute | solution.py:15
  60.4 4.2 constant_dynamic-update-slice_fusion
  66.1 44.7 %multiply_subtract_fusion.2 = f32[1,4,16,8192]{3,2,1,0:T(8,128)} fusion(f32[2,4,24,8192]{3,2,1,0:T(8,128)} %constant_dynamic-update-slice_fusion.2, f32[2,4,24,8192]{3,2,1,0:T(8,128)} %get-tuple-element.73, f32[2,4,16,8192]{3,2,1,0:T(8,128)S(1)} %copy-done, f32[16]{0:T(128)S(1)} %get-tuple-element.37, f32[16]{0:T(128)S(1)} %get-tuple-element.38, ...), kind=kLoop, calls=%fused_computation.11 | loop fusion | flops 35127296 | bytes 73402496 | tf_op jit(solution)/shard_map/sub | solution.py:72
  110.8 44.8 %multiply_add_fusion.2 = f32[1,4,16,8192]{3,2,1,0:T(8,128)} fusion(f32[2,4,24,8192]{3,2,1,0:T(8,128)} %constant_dynamic-update-slice_fusion.2, f32[2,4,24,8192]{3,2,1,0:T(8,128)} %get-tuple-element.73, f32[2,4,16,8192]{3,2,1,0:T(8,128)S(1)} %copy-done, f32[16]{0:T(128)S(1)} %get-tuple-element.37, f32[16]{0:T(128)S(1)} %get-tuple-element.38, ...), kind=kLoop, calls=%fused_computation.10 | loop fusion | flops 35127296 | bytes 73402496 | tf_op jit(solution)/shard_map/add | solution.py:73
  158.1 4.7 copy.126
  162.8 5.8 all-to-all-start
  169.3 46.1 %all-to-all-done = f32[2,4,16,8192]{3,1,0,2:T(4,128)} async-done(((f32[2,4,16,8192]{3,1,0,2:T(4,128)}), f32[2,4,16,8192]{3,1,0,2:T(4,128)}, u32[]{:S(2)}, u32[]{:S(2)}) %all-to-all-start) | async-done | bytes 4194336 | tf_op jit(solution)/shard_map/all_to_all | solution.py:75
  215.4 5.4 copy.224
  223.1 3.1 reshape_squeeze.7
  226.1 4.9 fusion.6
  231.0 4.2 reshape_squeeze.6
  235.2 5.4 fusion.8
  240.6 3.7 convolution_subtract_fusion
  244.3 3.6 convolution_add_fusion
  250.6 3.5 fusion.1
  254.1 3.7 add_bitcast_fusion
  257.8 2.7 stack.18
  260.5 5.8 subtract_bitcast_fusion
  266.3 2.9 stack.19
  269.2 3.9 maximum_multiply_fusion
  273.1 44.6 %copy.138 = f32[2,1,4,8,16384]{3,2,1,0,4:T(4,128)} copy(f32[2,1,4,8,16384]{4,3,2,1,0:T(8,128)} %maximum_multiply_fusion) | data formatting | bytes 8388608 | tf_op jit(solution)/shard_map/mul | solution.py:57
  317.7 82.5 %reshape.729 = f32[16,1,65536]{2,1,0:T(1,128)} reshape(f32[16384,2,1,4,8]{4,3,2,1,0:T(4,128)} %bitcast.180) | data formatting | bytes 8388608
  400.3 7.0 all-to-all-start.1
  408.0 35.1 %all-gather.2.cloned.1.call-done = f32[2,16,16,1024]{3,2,1,0:T(8,128)} async-done(((f32[2,8,16,1024]{3,2,1,0:T(8,128)}), f32[2,16,16,1024]{3,2,1,0:T(8,128)}) %all-gather.2.cloned.1.call-update) | async-done | bytes 2097168 | tf_op jit(solution)/shard_map/all_gather | solution.py:92
  443.1 2.7 convolution_bitcast_fusion
  448.2 53.3 %all-to-all-done.1 = f32[16,1,65536]{2,1,0:T(1,128)} async-done(((f32[16,1,65536]{2,1,0:T(1,128)}), f32[16,1,65536]{2,1,0:T(1,128)}, u32[]{:S(2)}, u32[]{:S(2)}) %all-to-all-start.1) | async-done | bytes 4194336 | tf_op jit(solution)/shard_map/all_to_all | solution.py:80
  502.1 13.7 %reduce.68 = f32[16,65536]{1,0:T(8,128)} reduce(f32[16,1,65536]{2,1,0:T(1,128)} %all-to-all-done.1, f32[]{:T(128)} %broadcast.1262), dimensions={1}, to_apply=%all_to_all.25.reduce_sub_computation | reduce | bytes 8388612 | tf_op jit(solution)/shard_map/all_to_all | solution.py:80
  515.8 109.0 %reshape.730 = f32[16384,2,1,4,8]{4,3,2,1,0:T(4,128)} reshape(f32[16,65536]{1,0:T(8,128)} %reduce.68) | data formatting | bytes 8388608
  624.8 53.3 %copy.158 = f32[2,1,4,8,16,1024]{5,3,2,4,0,1:T(8,128)} copy(f32[2,1,4,8,16,1024]{3,2,0,5,4,1:T(4,128)} %bitcast.17) | data formatting | bytes 8388608 | tf_op jit(solution)/shard_map/all_to_all | solution.py:80
  681.0 5.3 multiply_subtract_fusion
  686.3 5.3 multiply_add_fusion
  (57 shorter events, 24.5 us)
Async XLA Ops:
  6.5 8.9 %copy-start.7 = (f32[2,17,16]{1,2,0:T(8,128)S(1)}, f32[2,17,16]{1,2,0:T(8,128)}, u32[]{:S(2)}) copy-start(f32[2,17,16]{1,2,0:T(8,128)} %param.5) | copy-start | bytes 6532
  9.0 49.8 %collective-permute-start = (f32[2,4,8,8192]{3,2,1,0:T(8,128)S(1)}, f32[2,4,8,8192]{3,2,1,0:T(8,128)S(1)}, u32[]{:S(2)}, u32[]{:S(2)}) collective-permute-start(f32[2,4,8,8192]{3,2,1,0:T(8,128)S(1)} %get-tuple-element.75), channel_id=1, source_target_pairs={{0,1},{1,2},{2,3},{4,5},{5,6},{6,7},{8,9},{9,10},{10,11},{12,13},{... | collective-permute-start | bytes 6291464 | tf_op jit(solution)/shard_map/ppermute | solution.py:15
  14.1 50.5 %collective-permute-start.1 = (f32[2,4,8,8192]{3,2,1,0:T(8,128)S(1)}, f32[2,4,8,8192]{3,2,1,0:T(8,128)S(1)}, u32[]{:S(2)}, u32[]{:S(2)}) collective-permute-start(f32[2,4,8,8192]{3,2,1,0:T(8,128)S(1)} %get-tuple-element.76), channel_id=1, source_target_pairs={{1,0},{2,1},{3,2},{5,4},{6,5},{7,6},{9,8},{10,9},{11,10},{13,12},{... | collective-permute-start | bytes 6291464 | tf_op jit(solution)/shard_map/ppermute | solution.py:16
  16.4 44.0 %copy-start = (f32[2,4,16,8192]{3,2,1,0:T(8,128)S(1)}, f32[2,4,16,8192]{3,2,1,0:T(8,128)}, u32[]{:S(2)}) copy-start(f32[2,4,16,8192]{3,2,1,0:T(8,128)} %param.4) | copy-start | bytes 12582916
  162.8 52.6 %all-to-all-start = ((f32[2,4,16,8192]{3,1,0,2:T(4,128)}), f32[2,4,16,8192]{3,1,0,2:T(4,128)}, u32[]{:S(2)}, u32[]{:S(2)}) async-start(f32[2,4,16,8192]{3,1,0,2:T(4,128)} %copy.126), calls=%async_computation | async-start | bytes 8388608 | tf_op jit(solution)/shard_map/all_to_all | solution.py:75
  226.1 4.9 copy-start.2
  235.2 5.4 copy-start.4
  235.2 5.4 copy-start.5
  240.6 3.7 copy-start.3
  247.9 6.2 copy-start.1
  266.3 2.9 copy-start.6
  400.3 42.8 %copy-start.8 = (s32[16]{0:T(128)S(1)}, s32[16]{0:T(128)}, u32[]{:S(2)}) copy-start(s32[16]{0:T(128)} %param.7) | copy-start | bytes 196
  400.3 101.3 %all-to-all-start.1 = ((f32[16,1,65536]{2,1,0:T(1,128)}), f32[16,1,65536]{2,1,0:T(1,128)}, u32[]{:S(2)}, u32[]{:S(2)}) async-start(f32[16,1,65536]{2,1,0:T(1,128)} %reshape.729), calls=%async_computation.1 | async-start | bytes 8388608 | tf_op jit(solution)/shard_map/all_to_all | solution.py:80
  407.3 35.8 %all-gather.2.cloned.1.call-start = ((), (), s32[]{:S(2)}) async-start(), calls=%async_computation.2 | async-start | bytes 3145728 | tf_op jit(solution)/shard_map/all_gather | solution.py:92
Sparse Core Ops, SparseCore 0:
  409.6 33.4 all-gather.1
where the time goes:
time: 714 us; the launch traced here: 701 us
  local copies, waits for them, and re-layouts  331 us (46%)
  waiting for transfers between devices  178 us (25%)
  other arithmetic  123 us (17%)
  matrix products  35.9 us (5%)
  starting transfers between devices  19.2 us (3%)
  between operations  14 us (2%)
    unnamed x37, local copies, waits for them, and re-layouts  193 us
    all_to_all x2, local copies, waits for them, and re-layouts, shards(): lax.all_to_all(spectrum[:, None], ('chan', 'rng'), split_axis=4, concat_a...  53.9 us
    all_to_all x1, waiting for transfers between devices, shards(): lax.all_to_all(spectrum[:, None], ('chan', 'rng'), split_axis=4, concat_a...  53.3 us
    all_to_all x1, waiting for transfers between devices, shards(): lax.all_to_all(filtered, 'az', split_axis=2, concat_axis=3, tiled=True)  46.1 us
    add x1, other arithmetic, shards(): imag_part = imag_part + tap_real * seg_imag + tap_imag * seg_real  44.8 us
    sub x1, other arithmetic, shards(): real_part = real_part + tap_real * seg_real - tap_imag * seg_imag  44.7 us
    mul x1, local copies, waits for them, and re-layouts, azimuth_fft(): jnp.stack([out_real.reshape(lead + (count,)), out_imag.reshape(lead + (co...  44.6 us
    ppermute x1, waiting for transfers between devices, with_halo(): before = lax.ppermute(last, axis, up)  42.5 us
  transfers between devices with their start and end apart: 5, of which 4 were waited for; matrix products, arithmetic and copies ran while one was open for 2% of the time, Pallas kernels for 0%

commit v1 on v0

--- a/solution.py
+++ b/solution.py
@@ -3,6 +3,28 @@
 import jax.numpy as jnp
 from jax import lax
 from jax.sharding import PartitionSpec as P
+
+
+def in_blocks(x, dim, peers):
+    before, after = (x.shape[:dim], x.shape[dim + 1 :])
+    return jnp.moveaxis(x.reshape(*before, peers, -1, *after), dim, 0)
+
+
+def in_order(blocks, dim):
+    blocks = jnp.moveaxis(blocks, 0, dim)
+    dims = blocks.shape
+    return blocks.reshape(*dims[:dim], dims[dim] * dims[dim + 1], *dims[dim + 2 :])
+
+
+def swapped_with_each(x, axis, split_dim, concat_dim):
+    size, place = (lax.axis_size(axis), lax.axis_index(axis))
+    blocks = in_blocks(x, split_dim, size)
+    outs = [blocks[place]]
+    for hop in range(1, size):
+        sent = blocks[place ^ hop]
+        outs.append(lax.ppermute(sent, axis, [(i, i ^ hop) for i in range(size)]))
+    blocks = jnp.stack(outs)[place ^ jnp.arange(size)]
+    return in_order(blocks, concat_dim)
 
 
 def with_halo(shard, sides, width):
@@ -77,9 +99,7 @@
     groups = lax.axis_size("chan")
     local_channels = spectrum.shape[1]
     local_range = spectrum.shape[2]
-    moved = lax.all_to_all(
-        spectrum[:, None], ("chan", "rng"), split_axis=4, concat_axis=1, tiled=True
-    )
+    moved = swapped_with_each(spectrum[:, None], ("chan", "rng"), 4, 1)
     bins = moved.shape[-1]
     moved = moved.reshape((2, groups, strips, local_channels, local_range, bins))
     doppler = jnp.transpose(moved, (0, 1, 3, 2, 4, 5)).reshape(

time: 714 us -> 409 us (0.57)
  local copies, waits for them, and re-layouts: 331 us -> 75.2 us
  waiting for transfers between devices: 178 us -> 112 us
  starting transfers between devices: 19.2 us -> 56.8 us
  other arithmetic: 123 us -> 108 us
    unnamed x37 -> x91, local copies, waits for them, and re-layouts: 193 us -> 21.2 us
    all_to_all x2 -> x0, local copies, waits for them, and re-layouts: 53.9 us -> none  [shards(): lax.all_to_all(spectrum[:, None], ('chan', 'rng'), split_axis=4, concat_a...]
    all_to_all x1 -> x0, waiting for transfers between devices: 53.3 us -> none  [shards(): lax.all_to_all(spectrum[:, None], ('chan', 'rng'), split_axis=4, concat_a...]
    mul x1 -> x0, local copies, waits for them, and re-layouts: 44.6 us -> none  [azimuth_fft(): jnp.stack([out_real.reshape(lead + (count,)), out_imag.reshape(lead + (co...]
    ppermute x0 -> x15, starting transfers between devices: none -> 43.3 us  [swapped_with_each(): outs.append(lax.ppermute(sent, axis, [(i, i ^ hop) for i in range(size)]))]
    all_gather x1, waiting for transfers between devices: 35.1 us -> 0.02 us  [shards(): piece = lax.all_gather(recon, 'az', axis=1, tiled=True)]
    ppermute x0 -> x15, waiting for transfers between devices: none -> 34.4 us  [swapped_with_each(): outs.append(lax.ppermute(sent, axis, [(i, i ^ hop) for i in range(size)]))]
    all_to_all x1 -> x0, other arithmetic: 13.7 us -> none  [shards(): lax.all_to_all(spectrum[:, None], ('chan', 'rng'), split_axis=4, concat_a...]
  transfers between devices with their start and end apart: 5 -> 19, of which waited for: 4 -> 8; matrix products, arithmetic and copies ran while one was open for 2% -> 32% of each run, Pallas kernels for 0% -> 0%
where the time goes in v1:
time: 409 us; the launch traced here: 402 us
  waiting for transfers between devices  112 us (27%)
  other arithmetic  108 us (26%)
  local copies, waits for them, and re-layouts  75.2 us (18%)
  starting transfers between devices  56.8 us (14%)
  matrix products  35.6 us (9%)
  between operations  14.4 us (4%)
    add x1, other arithmetic, shards(): imag_part = imag_part + tap_real * seg_imag + tap_imag * seg_real  44.9 us
    sub x1, other arithmetic, shards(): real_part = real_part + tap_real * seg_real - tap_imag * seg_imag  44.8 us
    ppermute x15, starting transfers between devices, swapped_with_each(): outs.append(lax.ppermute(sent, axis, [(i, i ^ hop) for i in range(size)]))  43.3 us
    ppermute x1, waiting for transfers between devices, with_halo(): before = lax.ppermute(last, axis, up)  40.7 us
    all_to_all x1, waiting for transfers between devices, shards(): lax.all_to_all(filtered, 'az', split_axis=2, concat_axis=3, tiled=True)  36.9 us
    ppermute x15, waiting for transfers between devices, swapped_with_each(): outs.append(lax.ppermute(sent, axis, [(i, i ^ hop) for i in range(size)]))  34.4 us
    unnamed x91, local copies, waits for them, and re-layouts  21.2 us
  transfers between devices with their start and end apart: 19, of which 8 were waited for; matrix products, arithmetic and copies ran while one was open for 32% of the time, Pallas kernels for 0%

profile of v1, /device:TPU:0, one launch (start us, length us, event | category | flops | bytes accessed | tf_op | source)
XLA Modules:
  0.0 401.7 jit_solution(14900316004528743159)
XLA Ops:
  6.5 4.7 %fusion.72 = (f32[2,4,8,8192]{3,2,1,0:T(8,128)}, f32[2,4,8,8192]{3,2,1,0:T(8,128)}) fusion(f32[2,4,16,8192]{3,2,1,0:T(8,128)} %param.4), kind=kLoop, calls=%fused_computation.237 | loop fusion | bytes 8388608 | tf_op jit(solution)/shard_map/slice | solution.py:35
  11.2 6.3 %collective-permute-start = (f32[2,4,8,8192]{3,2,1,0:T(8,128)}, f32[2,4,8,8192]{3,2,1,0:T(8,128)}, u32[]{:S(2)}, u32[]{:S(2)}) collective-permute-start(f32[2,4,8,8192]{3,2,1,0:T(8,128)} %get-tuple-element.91), channel_id=1, source_target_pairs={{0,1},{1,2},{2,3},{4,5},{5,6},{6,7},{8,9},{9,10},{10,11},{12,13},{... | collective-permute-start | bytes 6291464 | tf_op jit(solution)/shard_map/ppermute | solution.py:37
  20.6 40.7 %collective-permute-done = f32[2,4,8,8192]{3,2,1,0:T(8,128)} collective-permute-done((f32[2,4,8,8192]{3,2,1,0:T(8,128)}, f32[2,4,8,8192]{3,2,1,0:T(8,128)}, u32[]{:S(2)}, u32[]{:S(2)}) %collective-permute-start) | collective-permute-done | bytes 2097184 | tf_op jit(solution)/shard_map/ppermute | solution.py:37
  61.3 3.1 constant_dynamic-update-slice_fusion.1
  64.4 4.2 %constant_dynamic-update-slice_fusion = (f32[2,4,24,8192]{3,2,1,0:T(8,128)}, f32[2,4,24,8192]{3,2,1,0:T(8,128)}) fusion(f32[2,4,24,8192]{3,2,1,0:T(8,128)} %constant_dynamic-update-slice_fusion.1, f32[2,4,16,8192]{3,2,1,0:T(8,128)S(1)} %copy-done), kind=kLoop, calls=%fused_computation.140 | loop fusion | bytes 12582912 | tf_op jit(solution)/shard_map/concatenate | solution.py:39
  68.6 3.0 constant_dynamic-update-slice_fusion.2
  71.7 44.9 %multiply_add_fusion.2 = f32[1,4,16,8192]{3,2,1,0:T(8,128)} fusion(f32[2,4,24,8192]{3,2,1,0:T(8,128)} %constant_dynamic-update-slice_fusion.2, f32[2,4,24,8192]{3,2,1,0:T(8,128)} %get-tuple-element.89, f32[2,4,16,8192]{3,2,1,0:T(8,128)S(1)} %copy-done, f32[16]{0:T(128)S(1)} %get-tuple-element.37, f32[16]{0:T(128)S(1)} %get-tuple-element.38, ...), kind=kLoop, calls=%fused_computation.11 | loop fusion | flops 35127296 | bytes 73402496 | tf_op jit(solution)/shard_map/add | solution.py:95
  116.6 44.8 %multiply_subtract_fusion.2 = f32[1,4,16,8192]{3,2,1,0:T(8,128)} fusion(f32[2,4,24,8192]{3,2,1,0:T(8,128)} %constant_dynamic-update-slice_fusion.2, f32[2,4,24,8192]{3,2,1,0:T(8,128)} %get-tuple-element.89, f32[2,4,16,8192]{3,2,1,0:T(8,128)S(1)} %copy-done, f32[16]{0:T(128)S(1)} %get-tuple-element.37, f32[16]{0:T(128)S(1)} %get-tuple-element.38, ...), kind=kLoop, calls=%fused_computation.12 | loop fusion | flops 35127296 | bytes 73402496 | tf_op jit(solution)/shard_map/sub | solution.py:94
  163.9 4.7 %copy.73 = f32[2,4,16,8192]{3,1,0,2:T(4,128)} copy(f32[2,4,16,8192]{3,2,1,0:T(8,128)S(1)} %pad_maximum_fusion) | data formatting | bytes 8388608 | tf_op jit(solution)/shard_map/stack | solution.py:96
  168.6 6.0 %all-to-all-start = ((f32[2,4,16,8192]{3,1,0,2:T(4,128)}), f32[2,4,16,8192]{3,1,0,2:T(4,128)}, u32[]{:S(2)}, u32[]{:S(2)}) async-start(f32[2,4,16,8192]{3,1,0,2:T(4,128)} %copy.73), calls=%async_computation | async-start | bytes 8388608 | tf_op jit(solution)/shard_map/all_to_all | solution.py:97
  184.4 36.9 %all-to-all-done = f32[2,4,16,8192]{3,1,0,2:T(4,128)} async-done(((f32[2,4,16,8192]{3,1,0,2:T(4,128)}), f32[2,4,16,8192]{3,1,0,2:T(4,128)}, u32[]{:S(2)}, u32[]{:S(2)}) %all-to-all-start) | async-done | bytes 4194336 | tf_op jit(solution)/shard_map/all_to_all | solution.py:97
  221.4 5.4 %copy.200 = f32[2,4,2,8,8192]{4,2,3,1,0:T(2,128)S(1)} copy(f32[2,4,2,8,8192]{4,1,0,3,2:T(4,128)} %bitcast.5) | data formatting | bytes 8388608 | tf_op jit(solution)/shard_map/all_to_all | solution.py:97
  229.1 3.1 reshape_squeeze.6
  232.2 4.8 %fusion.8 = f32[4,8,128,128]{3,2,1,0:T(8,128)} fusion(f32[4,8,128,128]{3,2,1,0:T(8,128)S(1)} %reshape_squeeze.6), kind=kOutput, calls=%fused_computation.124 | convolution fusion | flops 805535744 | bytes 4194304 | tf_op jit(solution)/shard_map/...ab,af->...bf/dot_general | solution.py:62
  237.0 3.5 reshape_squeeze.7
  241.8 3.6 fusion.6
  245.5 5.3 %convolution_add_fusion = f32[4,8,128,128]{3,2,1,0:T(8,128)S(1)} fusion(f32[4,8,128,128]{3,2,1,0:T(8,128)S(1)} %copy-done.5, f32[4,8,128,128]{3,2,1,0:T(8,128)} %copy-done.4), kind=kOutput, calls=%fused_computation.15 | convolution fusion | flops 806060032 | bytes 6291456 | tf_op jit(solution)/shard_map/...ab,af->...bf/dot_general | solution.py:62
  250.8 3.6 convolution_subtract_fusion
  256.9 3.5 fusion
  260.4 3.7 subtract_bitcast_fusion
  266.9 5.8 %add_bitcast_fusion = f32[4,8,128,128]{3,2,1,0:T(8,128)} fusion(f32[128,4,8,128]{3,0,2,1:T(8,128)} %fusion, f32[4,8,128,128]{3,2,1,0:T(8,128)S(1)} %convolution_add_fusion, f32[4,8,128,128]{3,2,1,0:T(8,128)} %copy-done.1, f32[128,128]{1,0:T(8,128)S(1)} %copy.84, f32[128,128]{1,0:T(8,128)S(1)} %copy.79), kind=kOutput, calls=%fused_computation.8 | convolution fusion | flops 807632896 | bytes 8519680 | tf_op jit(solution)/shard_map/...bf,bg->...gf/dot_general | solution.py:74
  277.6 5.3 %constant_dynamic-slice_fusion = (f32[2,1,4,8,1,1024]{5,4,3,2,1,0:T(1,128)S(1)}, f32[2,1,4,8,1,1024]{5,4,3,2,1,0:T(1,128)S(1)}, f32[2,1,4,8,1,1024]{5,4,3,2,1,0:...) fusion(f32[2,1,4,8,16,1024]{5,4,3,2,1,0:T(8,128)S(1)} %maximum_, ...), kind=kLoop, calls=%fused_computation.193 | loop fusion | bytes 8388672 | tf_op jit(solution)/shard_map/dynamic-slice.15
  290.9 4.5 %collective-permute-done.2 = f32[2,1,4,8,1024]{4,3,2,0,1:T(8,128)S(1)} collective-permute-done((f32[2,1,4,8,1024]{4,3,2,0,1:T(8,128)S(1)}, f32[2,1,4,8,1024]{4,3,2,0,1:T(8,128)S(1)}, u32[]{:S(2)}, u32[]{:S(2)}) %collective-permute-start.2) | collective-permute-done | bytes 262176 | tf_op jit(solution)/shard_map/ppermute | solution.py:25
  296.1 10.8 %collective-permute-done.3 = f32[2,1,4,8,1024]{4,3,2,0,1:T(8,128)S(1)} collective-permute-done((f32[2,1,4,8,1024]{4,3,2,0,1:T(8,128)S(1)}, f32[2,1,4,8,1024]{4,3,2,0,1:T(8,128)S(1)}, u32[]{:S(2)}, u32[]{:S(2)}) %collective-permute-start.3) | collective-permute-done | bytes 262176 | tf_op jit(solution)/shard_map/ppermute | solution.py:25
  309.9 19.1 %collective-permute-start.10 = (f32[2,1,4,8,1024]{4,3,2,0,1:T(8,128)S(1)}, f32[2,1,4,8,1024]{4,3,2,0,1:T(8,128)S(1)}, u32[]{:S(2)}, u32[]{:S(2)}) collective-permute-start(f32[2,1,4,8,1024]{4,3,2,0,1:T(8,128)S(1)} %bitcast.276), channel_id=1, source_target_pairs={{0,17},{1,16},{2,19},{3,18},{8,25},{9,24},{10,27},{11,26},{16,1},{... | collective-permute-start | bytes 786440 | tf_op jit(solution)/shard_map/ppermute | solution.py:25
  336.2 11.4 %collective-permute-start.14 = (f32[2,1,4,8,1024]{4,3,2,0,1:T(8,128)S(1)}, f32[2,1,4,8,1024]{4,3,2,0,1:T(8,128)S(1)}, u32[]{:S(2)}, u32[]{:S(2)}) collective-permute-start(f32[2,1,4,8,1024]{4,3,2,0,1:T(8,128)S(1)} %bitcast.272), channel_id=1, source_target_pairs={{0,25},{1,24},{2,27},{3,26},{8,17},{9,16},{10,19},{11,18},{16,9},{... | collective-permute-start | bytes 786440 | tf_op jit(solution)/shard_map/ppermute | solution.py:25
  349.5 3.0 collective-permute-done.11
  354.0 7.7 %collective-permute-done.13 = f32[2,1,4,8,1024]{4,3,2,0,1:T(8,128)S(1)} collective-permute-done((f32[2,1,4,8,1024]{4,3,2,0,1:T(8,128)S(1)}, f32[2,1,4,8,1024]{4,3,2,0,1:T(8,128)S(1)}, u32[]{:S(2)}, u32[]{:S(2)}) %collective-permute-start.13) | collective-permute-done | bytes 262176 | tf_op jit(solution)/shard_map/ppermute | solution.py:25
  364.6 7.7 %collective-permute-done.16 = f32[2,1,4,8,1024]{4,3,2,0,1:T(8,128)S(1)} collective-permute-done((f32[2,1,4,8,1024]{4,3,2,0,1:T(8,128)S(1)}, f32[2,1,4,8,1024]{4,3,2,0,1:T(8,128)S(1)}, u32[]{:S(2)}, u32[]{:S(2)}) %collective-permute-start.16) | collective-permute-done | bytes 262176 | tf_op jit(solution)/shard_map/ppermute | solution.py:25
  373.0 4.9 %gather_fusion = f32[16,2,4,8,1024]{4,3,2,1,0:T(8,128)} fusion(f32[16,2,4,8,1024]{4,3,2,1,0:T(8,128)} %bitcast.32, s32[1024]{0:T(1024)S(1)} %pad_clamp_fusion), kind=kCustom, calls=%fused_computation | custom fusion | bytes 8388672 | tf_op jit(solution)/shard_map/gather | solution.py:26
  381.7 5.2 %multiply_add_fusion = f32[1,16,4,8,1024]{4,3,2,1,0:T(8,128)S(1)} fusion(f32[4,8,1024]{2,1,0:T(8,128)S(1)} %get-tuple-element.40, f32[16,1024]{1,0:T(8,128)S(1)} %get-tuple-element.125, f32[4,8,1024]{2,1,0:T(8,128)S(1)} %get-tuple-element.41, f32[16,1024]{1,0:T(8,128)S(1)} %get-tuple-element.126, f32[4,8,1024]{2,1,0:T(8,128)S(1)} %get-tuple-element.42, ...), kind=kLoop, calls=%fused_computation.5 | loop fusion | flops 33030144 | bytes 8388608 | tf_op jit(solution)/shard_map/add | solution.py:123
  387.0 5.3 %multiply_subtract_fusion = f32[1,16,4,8,1024]{4,3,2,1,0:T(8,128)S(1)} fusion(f32[4,8,1024]{2,1,0:T(8,128)S(1)} %get-tuple-element.40, f32[16,1024]{1,0:T(8,128)S(1)} %get-tuple-element.125, f32[4,8,1024]{2,1,0:T(8,128)S(1)} %get-tuple-element.41, f32[16,1024]{1,0:T(8,128)S(1)} %get-tuple-element.126, f32[4,8,1024]{2,1,0:T(8,128)S(1)} %get-tuple-element.42, ...), kind=kLoop, calls=%fused_computation.6 | loop fusion | flops 33030144 | bytes 8388608 | tf_op jit(solution)/shard_map/sub | solution.py:122
  (140 shorter events, 60.7 us)
Async XLA Ops:
  6.5 12.8 %copy-start.7 = (f32[2,17,16]{1,2,0:T(8,128)S(1)}, f32[2,17,16]{1,2,0:T(8,128)}, u32[]{:S(2)}) copy-start(f32[2,17,16]{1,2,0:T(8,128)} %param.5) | copy-start | bytes 6532
  6.5 168.1 %all-gather.2.cloned.1.call-start = ((), (), s32[]{:S(2)}) async-start(), calls=%async_computation.1 | async-start | bytes 3145728 | tf_op jit(solution)/shard_map/all_gather | solution.py:112
  11.2 50.1 %collective-permute-start = (f32[2,4,8,8192]{3,2,1,0:T(8,128)}, f32[2,4,8,8192]{3,2,1,0:T(8,128)}, u32[]{:S(2)}, u32[]{:S(2)}) collective-permute-start(f32[2,4,8,8192]{3,2,1,0:T(8,128)} %get-tuple-element.91), channel_id=1, source_target_pairs={{0,1},{1,2},{2,3},{4,5},{5,6},{6,7},{8,9},{9,10},{10,11},{12,13},{... | collective-permute-start | bytes 6291464 | tf_op jit(solution)/shard_map/ppermute | solution.py:37
  17.5 51.1 %collective-permute-start.1 = (f32[2,4,8,8192]{3,2,1,0:T(8,128)}, f32[2,4,8,8192]{3,2,1,0:T(8,128)}, u32[]{:S(2)}, u32[]{:S(2)}) collective-permute-start(f32[2,4,8,8192]{3,2,1,0:T(8,128)} %get-tuple-element.92), channel_id=1, source_target_pairs={{1,0},{2,1},{3,2},{5,4},{6,5},{7,6},{9,8},{10,9},{11,10},{13,12},{... | collective-permute-start | bytes 6291464 | tf_op jit(solution)/shard_map/ppermute | solution.py:38
  20.6 43.8 %copy-start = (f32[2,4,16,8192]{3,2,1,0:T(8,128)S(1)}, f32[2,4,16,8192]{3,2,1,0:T(8,128)}, u32[]{:S(2)}) copy-start(f32[2,4,16,8192]{3,2,1,0:T(8,128)} %param.4) | copy-start | bytes 12582916
  168.6 6.0 %copy-start.21 = (s32[16]{0:T(128)S(1)}, s32[16]{0:T(128)}, u32[]{:S(2)}) copy-start(s32[16]{0:T(128)} %param.7) | copy-start | bytes 196
  168.6 52.8 %all-to-all-start = ((f32[2,4,16,8192]{3,1,0,2:T(4,128)}), f32[2,4,16,8192]{3,1,0,2:T(4,128)}, u32[]{:S(2)}, u32[]{:S(2)}) async-start(f32[2,4,16,8192]{3,1,0,2:T(4,128)} %copy.73), calls=%async_computation | async-start | bytes 8388608 | tf_op jit(solution)/shard_map/all_to_all | solution.py:97
  232.2 4.9 %copy-start.2 = (f32[4,8,128,128]{3,2,1,0:T(8,128)}, f32[4,8,128,128]{3,2,1,0:T(8,128)S(1)}, u32[]{:S(2)}) copy-start(f32[4,8,128,128]{3,2,1,0:T(8,128)S(1)} %reshape_squeeze.6) | copy-start | bytes 6291460
  240.5 1.3 copy-start.4
  241.8 3.6 copy-start.5
  245.5 5.3 %copy-start.3 = (f32[4,8,128,128]{3,2,1,0:T(8,128)S(1)}, f32[4,8,128,128]{3,2,1,0:T(8,128)}, u32[]{:S(2)}) copy-start(f32[4,8,128,128]{3,2,1,0:T(8,128)} %copy-done.2) | copy-start | bytes 6291460
  254.4 6.0 %copy-start.1 = (f32[4,8,128,128]{3,2,1,0:T(8,128)}, f32[4,8,128,128]{3,2,1,0:T(8,128)S(1)}, u32[]{:S(2)}) copy-start(f32[4,8,128,128]{3,2,1,0:T(8,128)S(1)} %convolution_subtract_fusion) | copy-start | bytes 6291460
  272.6 2.8 copy-start.6
  277.6 7.9 %copy-start.19 = (f32[1,16,1,1024]{3,2,1,0:T(1,128)S(1)}, f32[1,16,1,1024]{3,2,1,0:T(1,128)}, u32[]{:S(2)}) copy-start(f32[1,16,1,1024]{3,2,1,0:T(1,128)} %get-tuple-element.93) | copy-start | bytes 196612
  277.6 7.9 %copy-start.20 = (f32[1,16,1,1024]{3,2,1,0:T(1,128)S(1)}, f32[1,16,1,1024]{3,2,1,0:T(1,128)}, u32[]{:S(2)}) copy-start(f32[1,16,1,1024]{3,2,1,0:T(1,128)} %get-tuple-element.112) | copy-start | bytes 196612
  282.9 12.5 %collective-permute-start.2 = (f32[2,1,4,8,1024]{4,3,2,0,1:T(8,128)S(1)}, f32[2,1,4,8,1024]{4,3,2,0,1:T(8,128)S(1)}, u32[]{:S(2)}, u32[]{:S(2)}) collective-permute-start(f32[2,1,4,8,1024]{4,3,2,0,1:T(8,128)S(1)} %bitcast.283), channel_id=1, source_target_pairs={{0,1},{1,0},{2,3},{3,2},{8,9},{9,8},{10,11},{11,10},{16,17},{17,16... | collective-permute-start | bytes 786440 | tf_op jit(solution)/shard_map/ppermute | solution.py:25
  285.6 21.4 %collective-permute-start.3 = (f32[2,1,4,8,1024]{4,3,2,0,1:T(8,128)S(1)}, f32[2,1,4,8,1024]{4,3,2,0,1:T(8,128)S(1)}, u32[]{:S(2)}, u32[]{:S(2)}) collective-permute-start(f32[2,1,4,8,1024]{4,3,2,0,1:T(8,128)S(1)} %bitcast.284), channel_id=1, source_target_pairs={{0,2},{1,3},{2,0},{3,1},{8,10},{9,11},{10,8},{11,9},{16,18},{17,19... | collective-permute-start | bytes 786440 | tf_op jit(solution)/shard_map/ppermute | solution.py:25
  289.0 18.6 %collective-permute-start.4 = (f32[2,1,4,8,1024]{4,3,2,0,1:T(8,128)S(1)}, f32[2,1,4,8,1024]{4,3,2,0,1:T(8,128)S(1)}, u32[]{:S(2)}, u32[]{:S(2)}) collective-permute-start(f32[2,1,4,8,1024]{4,3,2,0,1:T(8,128)S(1)} %bitcast.282), channel_id=1, source_target_pairs={{0,3},{1,2},{2,1},{3,0},{8,11},{9,10},{10,9},{11,8},{16,19},{17,18... | collective-permute-start | bytes 786440 | tf_op jit(solution)/shard_map/ppermute | solution.py:25
  289.2 20.7 %collective-permute-start.5 = (f32[2,1,4,8,1024]{4,3,2,0,1:T(8,128)S(1)}, f32[2,1,4,8,1024]{4,3,2,0,1:T(8,128)S(1)}, u32[]{:S(2)}, u32[]{:S(2)}) collective-permute-start(f32[2,1,4,8,1024]{4,3,2,0,1:T(8,128)S(1)} %bitcast.281), channel_id=1, source_target_pairs={{0,8},{1,9},{2,10},{3,11},{8,0},{9,1},{10,2},{11,3},{16,24},{17,25... | collective-permute-start | bytes 786440 | tf_op jit(solution)/shard_map/ppermute | solution.py:25
  289.3 40.5 %collective-permute-start.6 = (f32[2,1,4,8,1024]{4,3,2,0,1:T(8,128)S(1)}, f32[2,1,4,8,1024]{4,3,2,0,1:T(8,128)S(1)}, u32[]{:S(2)}, u32[]{:S(2)}) collective-permute-start(f32[2,1,4,8,1024]{4,3,2,0,1:T(8,128)S(1)} %bitcast.280), channel_id=1, source_target_pairs={{0,9},{1,8},{2,11},{3,10},{8,1},{9,0},{10,3},{11,2},{16,25},{17,24... | collective-permute-start | bytes 786440 | tf_op jit(solution)/shard_map/ppermute | solution.py:25
  295.4 35.6 %collective-permute-start.7 = (f32[2,1,4,8,1024]{4,3,2,0,1:T(8,128)S(1)}, f32[2,1,4,8,1024]{4,3,2,0,1:T(8,128)S(1)}, u32[]{:S(2)}, u32[]{:S(2)}) collective-permute-start(f32[2,1,4,8,1024]{4,3,2,0,1:T(8,128)S(1)} %bitcast.279), channel_id=1, source_target_pairs={{0,10},{1,11},{2,8},{3,9},{8,2},{9,3},{10,0},{11,1},{16,26},{17,27... | collective-permute-start | bytes 786440 | tf_op jit(solution)/shard_map/ppermute | solution.py:25
  307.0 27.5 %collective-permute-start.8 = (f32[2,1,4,8,1024]{4,3,2,0,1:T(8,128)S(1)}, f32[2,1,4,8,1024]{4,3,2,0,1:T(8,128)S(1)}, u32[]{:S(2)}, u32[]{:S(2)}) collective-permute-start(f32[2,1,4,8,1024]{4,3,2,0,1:T(8,128)S(1)} %bitcast.278), channel_id=1, source_target_pairs={{0,11},{1,10},{2,9},{3,8},{8,3},{9,2},{10,1},{11,0},{16,27},{17,26... | collective-permute-start | bytes 786440 | tf_op jit(solution)/shard_map/ppermute | solution.py:25
  307.7 28.5 %collective-permute-start.9 = (f32[2,1,4,8,1024]{4,3,2,0,1:T(8,128)S(1)}, f32[2,1,4,8,1024]{4,3,2,0,1:T(8,128)S(1)}, u32[]{:S(2)}, u32[]{:S(2)}) collective-permute-start(f32[2,1,4,8,1024]{4,3,2,0,1:T(8,128)S(1)} %bitcast.277), channel_id=1, source_target_pairs={{0,16},{1,17},{2,18},{3,19},{8,24},{9,25},{10,26},{11,27},{16,0},{... | collective-permute-start | bytes 786440 | tf_op jit(solution)/shard_map/ppermute | solution.py:25
  309.9 38.4 %collective-permute-start.10 = (f32[2,1,4,8,1024]{4,3,2,0,1:T(8,128)S(1)}, f32[2,1,4,8,1024]{4,3,2,0,1:T(8,128)S(1)}, u32[]{:S(2)}, u32[]{:S(2)}) collective-permute-start(f32[2,1,4,8,1024]{4,3,2,0,1:T(8,128)S(1)} %bitcast.276), channel_id=1, source_target_pairs={{0,17},{1,16},{2,19},{3,18},{8,25},{9,24},{10,27},{11,26},{16,1},{... | collective-permute-start | bytes 786440 | tf_op jit(solution)/shard_map/ppermute | solution.py:25
  329.8 22.7 %collective-permute-start.11 = (f32[2,1,4,8,1024]{4,3,2,0,1:T(8,128)S(1)}, f32[2,1,4,8,1024]{4,3,2,0,1:T(8,128)S(1)}, u32[]{:S(2)}, u32[]{:S(2)}) collective-permute-start(f32[2,1,4,8,1024]{4,3,2,0,1:T(8,128)S(1)} %bitcast.275), channel_id=1, source_target_pairs={{0,18},{1,19},{2,16},{3,17},{8,26},{9,27},{10,24},{11,25},{16,2},{... | collective-permute-start | bytes 786440 | tf_op jit(solution)/shard_map/ppermute | solution.py:25
  331.0 22.3 %collective-permute-start.12 = (f32[2,1,4,8,1024]{4,3,2,0,1:T(8,128)S(1)}, f32[2,1,4,8,1024]{4,3,2,0,1:T(8,128)S(1)}, u32[]{:S(2)}, u32[]{:S(2)}) collective-permute-start(f32[2,1,4,8,1024]{4,3,2,0,1:T(8,128)S(1)} %bitcast.274), channel_id=1, source_target_pairs={{0,19},{1,18},{2,17},{3,16},{8,27},{9,26},{10,25},{11,24},{16,3},{... | collective-permute-start | bytes 786440 | tf_op jit(solution)/shard_map/ppermute | solution.py:25
  334.5 27.3 %collective-permute-start.13 = (f32[2,1,4,8,1024]{4,3,2,0,1:T(8,128)S(1)}, f32[2,1,4,8,1024]{4,3,2,0,1:T(8,128)S(1)}, u32[]{:S(2)}, u32[]{:S(2)}) collective-permute-start(f32[2,1,4,8,1024]{4,3,2,0,1:T(8,128)S(1)} %bitcast.273), channel_id=1, source_target_pairs={{0,24},{1,25},{2,26},{3,27},{8,16},{9,17},{10,18},{11,19},{16,8},{... | collective-permute-start | bytes 786440 | tf_op jit(solution)/shard_map/ppermute | solution.py:25
  336.2 26.3 %collective-permute-start.14 = (f32[2,1,4,8,1024]{4,3,2,0,1:T(8,128)S(1)}, f32[2,1,4,8,1024]{4,3,2,0,1:T(8,128)S(1)}, u32[]{:S(2)}, u32[]{:S(2)}) collective-permute-start(f32[2,1,4,8,1024]{4,3,2,0,1:T(8,128)S(1)} %bitcast.272), channel_id=1, source_target_pairs={{0,25},{1,24},{2,27},{3,26},{8,17},{9,16},{10,19},{11,18},{16,9},{... | collective-permute-start | bytes 786440 | tf_op jit(solution)/shard_map/ppermute | solution.py:25
  348.3 15.5 %collective-permute-start.15 = (f32[2,1,4,8,1024]{4,3,2,0,1:T(8,128)S(1)}, f32[2,1,4,8,1024]{4,3,2,0,1:T(8,128)S(1)}, u32[]{:S(2)}, u32[]{:S(2)}) collective-permute-start(f32[2,1,4,8,1024]{4,3,2,0,1:T(8,128)S(1)} %bitcast.271), channel_id=1, source_target_pairs={{0,26},{1,27},{2,24},{3,25},{8,18},{9,19},{10,16},{11,17},{16,10},... | collective-permute-start | bytes 786440 | tf_op jit(solution)/shard_map/ppermute | solution.py:25
  352.5 19.8 %collective-permute-start.16 = (f32[2,1,4,8,1024]{4,3,2,0,1:T(8,128)S(1)}, f32[2,1,4,8,1024]{4,3,2,0,1:T(8,128)S(1)}, u32[]{:S(2)}, u32[]{:S(2)}) collective-permute-start(f32[2,1,4,8,1024]{4,3,2,0,1:T(8,128)S(1)} %bitcast.270), channel_id=1, source_target_pairs={{0,27},{1,26},{2,25},{3,24},{8,19},{9,18},{10,17},{11,16},{16,11},... | collective-permute-start | bytes 786440 | tf_op jit(solution)/shard_map/ppermute | solution.py:25
  380.7 1.0 copy-start.17
  380.7 1.1 copy-start.18
  (9 other events, 8.4 us)
Sparse Core Ops, SparseCore 0:
  18.9 35.4 all-gather.1
